TPU v7x, 32 devices: a whole 2x2x4 slice. The times are simulated.
32 devices in a mesh: row: 4 (over y, x), col: 8 (over z, core).
Axes of the slice: x: 2, y: 2, z: 4, core: 2. Of those that a mesh axis runs over, the one named last changes fastest.
Arguments:
- parent_front: bfloat16 [28672, 28672], P('row', 'col'), may hold values from -6 to 6
- child_update: bfloat16 [2, 14336, 14336], P(None, 'row', 'col'), may hold values from -6 to 6
- parent_test: bfloat16 [28672, 448], P('col'), may hold values from -0.03125 to 0.03125
- child_test: bfloat16 [2, 14336, 448], P(None, 'col'), may hold values from -0.046875 to 0.046875
- child_map: int32 [2, 112], replicated, may hold values from 0 to 223, as said below
Outputs:
- leaf_basis: bfloat16 [224, 128, 448], P('row', 'col')
- couplings: float32 [32, 448, 448], P('row', 'col')
Inputs may be any that keep to these rules, and one draw needn't show every extreme that they name: `child_map`: for each child the entries rise strictly along its blocks, and entry j is at least j.
All inputs are finite; a program needn't handle non-finite values.
Results may differ from a plain program's by a relative error of at most 0.006.
Values may be sent and summed in bfloat16 or wider, within the bound.
A program may use at most 192 MiB of HBM per device.

v0:
```python
import math
import jax
import jax.numpy as jnp
from jax import lax
from jax.sharding import PartitionSpec as P

LEAF = 896
BLOCK = 128
HIGH = lax.Precision.HIGHEST


def spread(block, axis, holder):
    block = jnp.where(lax.axis_index(axis) == holder, block, jnp.zeros_like(block))
    return lax.psum(block, axis)


def finish(leaves, gram_matrix):
    factor = jnp.linalg.cholesky(gram_matrix)
    solved = lax.linalg.triangular_solve(
        factor, leaves, left_side=False, lower=True, transpose_a=True
    )
    return (solved * math.sqrt(LEAF)).astype(jnp.bfloat16)


def local(parent_front, child_update, parent_test, child_test, child_map):
    row_count = lax.axis_size("row")
    col_count = lax.axis_size("col")
    row_index = lax.axis_index("row")
    col_index = lax.axis_index("col")
    slab_rows = BLOCK // col_count
    own_blocks = parent_front.shape[0] // BLOCK
    kid_blocks = child_update.shape[1] // BLOCK
    probes = parent_test.shape[1]
    own_probe = jnp.dot(parent_front, parent_test, preferred_element_type=jnp.float32)
    own_probe = own_probe.reshape(own_blocks, BLOCK, probes)
    kid_probe = jnp.stack(
        [
            jnp.dot(child_update[which], child_test[which], preferred_element_type=jnp.float32)
            for which in range(2)
        ]
    )
    kid_probe = kid_probe.reshape(2, kid_blocks, BLOCK, probes)
    own_share, kid_share = (
        lax.psum_scatter(own_probe, "col", scatter_dimension=1, tiled=True),
        lax.psum_scatter(kid_probe, "col", scatter_dimension=2, tiled=True),
    )
    first_block = row_index * own_blocks
    targets = jnp.arange(own_blocks, dtype=jnp.int32)
    mapped = child_map - first_block
    onehot = (mapped[:, None, :] == targets[None, :, None]).astype(jnp.float32)
    sample = own_share + jnp.einsum(
        "cpn,cnsr->psr",
        onehot,
        lax.all_gather(kid_share, "row", axis=1, tiled=True),
        precision=HIGH,
    )
    per_leaf = LEAF // BLOCK
    leaf_count = own_blocks // per_leaf
    leaves = sample.reshape(leaf_count, per_leaf * slab_rows, probes)
    partial_gram = jnp.einsum("lkr,lks->lrs", leaves, leaves, precision=HIGH)
    gram_matrix = lax.psum(partial_gram, "col")
    leaf_basis = finish(leaves, gram_matrix).reshape(own_blocks, slab_rows, probes)
    whole_basis = lax.all_gather(leaf_basis, "col", axis=1, tiled=True)
    bases = whole_basis.reshape(leaf_count, LEAF, probes)
    col_leaves = parent_front.shape[1] // LEAF
    shrink = 1.0 / math.sqrt(LEAF)

    def sibling_product(position):
        leaf_index = col_index * col_leaves + position
        sibling = jnp.bitwise_xor(leaf_index, 1)
        row_start = leaf_index % leaf_count * LEAF
        col_start = (sibling - col_index * col_leaves) * LEAF
        front_tile = lax.dynamic_slice(parent_front, (row_start, col_start), (LEAF, LEAF))
        product = (
            jnp.dot(front_tile, bases[sibling % leaf_count], preferred_element_type=jnp.float32)
            * shrink
        )
        return product.astype(jnp.bfloat16)

    products = lax.map(sibling_product, jnp.arange(col_leaves, dtype=jnp.int32))
    owner_span = col_count // row_count
    core_rows = probes // col_count
    received = [
        spread(products, "col", row_index * owner_span + offset) for offset in range(owner_span)
    ]
    products_all = jnp.concatenate(received, axis=0)
    columns = lax.dynamic_slice_in_dim(bases, col_index * core_rows, core_rows, 2)
    couplings = (
        jnp.einsum("lkr,lks->lrs", columns, products_all, preferred_element_type=jnp.float32)
        * shrink
    )
    return (leaf_basis, couplings)


def solution(mesh):
    in_specs = (P("row", "col"), P(None, "row", "col"), P("col", None), P(None, "col", None), P())
    out_specs = (P("row", "col", None), P("row", "col", None))
    return jax.shard_map(local, mesh=mesh, in_specs=in_specs, out_specs=out_specs, check_vma=False)
```

profile of v0, /device:TPU:0, one launch (start us, length us, event | category | flops | bytes accessed | tf_op | source)
XLA Modules:
  0.0 1988.0 jit_solution(7997422557833170795)
XLA Ops:
  16.7 10.6 convolution_bitcast_fusion.1
  27.3 10.6 convolution_bitcast_fusion.2
  37.8 10.9 pad_maximum_fusion
  48.7 21.7 %copy.91 = f32[2,28,128,448]{3,0,1,2:T(2,128)} copy(f32[2,28,128,448]{2,3,1,0:T(8,128)} %pad_maximum_fusion) | data formatting | bytes 25690112 | tf_op jit(solution)/shard_map/stack | solution.py:36
  72.3 295.1 %all-reduce.11.cloned.1.call-done = f32[2,28,128,448]{3,0,1,2:T(2,128)} async-done(((f32[2,28,128,448]{3,0,1,2:T(2,128)}), f32[2,28,128,448]{3,0,1,2:T(2,128)}) %all-reduce.11.cloned.1.call-update) | async-done | bytes 12845072
  372.4 30.3 %convolution_bitcast_fusion = f32[56,8,56,128]{3,1,2,0:T(8,128)} fusion(bf16[7168,3584]{1,0:T(8,128)(2,1)} %param.7, bf16[3584,448]{0,1:T(8,128)(2,1)S(1)} %copy-done), kind=kOutput, calls=%fused_computation.11 | convolution fusion | flops 23018340352 | bytes 67436544 | tf_op jit(solution)/shard_map/dot_general | solution.py:34
  402.7 12.1 copy.136
  414.8 16.4 copy.90
  431.9 19.0 all-gather.3.cloned.1.call-done
  450.9 151.3 %reduce-scatter.2.cloned.1.call-done = f32[56,16,448]{2,0,1:T(8,128)} async-done(((f32[56,128,448]{2,0,1:T(8,128)}), f32[56,16,448]{2,0,1:T(8,128)}) %reduce-scatter.2.cloned.1.call-update) | async-done | bytes 1605648 | tf_op jit(solution)/shard_map/reduce_scatter | solution.py:44
  602.2 10.3 bitcast_add_fusion.1
  623.1 153.0 %all-reduce.9.cloned.1.call-done = f32[8,448,448]{1,2,0:T(8,128)} async-done(((f32[8,448,448]{1,2,0:T(8,128)}), f32[8,448,448]{1,2,0:T(8,128)}) %all-reduce.9.cloned.1.call-update) | async-done | bytes 6422544 | tf_op jit(solution)/shard_map/psum | solution.py:61
  794.6 93.8 %custom-call.34 = f32[8,128,128]{2,1,0:T(8,128)S(1)} custom-call(f32[8,128,128]{2,1,0:T(8,128)S(1)} %cholesky.281), custom_call_target="Cholesky" | custom-call | tf_op jit(solution)/shard_map/jit(cholesky)/cholesky | solution.py:18
  892.4 79.2 %custom-call.35 = f32[8,1,128,128]{2,3,1,0:T(8,128)} custom-call(f32[8,1,128,128]{3,2,1,0:T(8,128)S(1)} %select_bitcast_fusion.2), custom_call_target="InvertDiagBlocksLowerTriangular" | custom-call | tf_op jit(solution)/shard_map/jit(cholesky)/cholesky | solution.py:18
  979.3 94.2 %custom-call.36 = f32[8,128,128]{2,1,0:T(8,128)S(1)} custom-call(f32[8,128,128]{2,1,0:T(8,128)S(1)} %cholesky.285), custom_call_target="Cholesky" | custom-call | tf_op jit(solution)/shard_map/jit(cholesky)/cholesky | solution.py:18
  1074.5 79.2 %custom-call.37 = f32[8,1,128,128]{2,3,1,0:T(8,128)} custom-call(f32[8,1,128,128]{3,2,1,0:T(8,128)S(1)} %get-tuple-element.154), custom_call_target="InvertDiagBlocksLowerTriangular" | custom-call | tf_op jit(solution)/shard_map/jit(cholesky)/cholesky | solution.py:18
  1161.3 95.4 %custom-call.38 = f32[8,128,128]{2,1,0:T(8,128)} custom-call(f32[8,128,128]{2,1,0:T(8,128)} %cholesky.290), custom_call_target="Cholesky" | custom-call | tf_op jit(solution)/shard_map/jit(cholesky)/cholesky | solution.py:18
  1259.1 79.4 %custom-call.39 = f32[8,1,128,128]{2,3,1,0:T(8,128)S(1)} custom-call(f32[8,1,128,128]{3,2,1,0:T(8,128)} %get-tuple-element.152), custom_call_target="InvertDiagBlocksLowerTriangular" | custom-call | tf_op jit(solution)/shard_map/jit(cholesky)/cholesky | solution.py:18
  1342.4 46.9 %custom-call.40 = f32[8,64,64]{2,1,0:T(8,128)S(1)} custom-call(f32[8,64,64]{2,1,0:T(8,128)S(1)} %convolution_subtract_fusion.3), custom_call_target="Cholesky" | custom-call | tf_op jit(solution)/shard_map/jit(cholesky)/cholesky | solution.py:18
  1397.7 12.5 while.16
  1413.5 316.0 %custom-call.41 = f32[8,4,128,128]{2,3,1,0:T(8,128)} custom-call(f32[8,4,128,128]{3,2,1,0:T(8,128)} %pad_maximum_fusion.1), custom_call_target="InvertDiagBlocksLowerTriangular" | custom-call | tf_op jit(solution)/shard_map/triangular_solve | solution.py:19
  1742.5 73.5 %all-gather.5.cloned.1.call-done = bf16[56,128,448]{2,1,0:T(8,128)(2,1)} async-done(((bf16[56,16,448]{2,1,0:T(8,128)(2,1)}), bf16[56,128,448]{2,1,0:T(8,128)(2,1)}) %all-gather.5.cloned.1.call-update) | async-done | bytes 6422544 | tf_op jit(solution)/shard_map/all_gather | solution.py:63
  1816.0 17.0 while.15
  1836.2 137.2 %all-reduce.13.cloned.1.call-done = (bf16[4,896,448]{1,2,0:T(8,128)(2,1)}, bf16[4,896,448]{1,2,0:T(8,128)(2,1)}) async-done(((bf16[4,896,448]{1,2,0:T(8,128)(2,1)}, bf16[4,896,448]{1,2,0:T(8,128)(2,1)}), (bf16[4,896,448]{1,2,0:T(8,128)(2,1)}, bf16[4,896,448]{1,2,0:T(8,128)(2,1)})) %all-reduce.13.cloned.1.call-update) | async-done | bytes 6422544 | tf_op jit(solution)/shard_map/psum | solution.py:14
  (106 shorter events, 133.5 us)
Async XLA Ops:
  7.2 365.2 %copy-start = (bf16[3584,448]{0,1:T(8,128)(2,1)S(1)}, bf16[3584,448]{0,1:T(8,128)(2,1)}, u32[]{:S(2)}) copy-start(bf16[3584,448]{0,1:T(8,128)(2,1)} %param.9) | copy-start | bytes 9633796
  7.2 360.2 %all-reduce.11.cloned.1.call-start = ((), (), s32[]{:S(2)}) async-start(), calls=%async_computation.5 | async-start | bytes 29360128
  70.4 0.7 copy-start.10
  70.4 380.5 %all-gather.3.cloned.1.call-start = ((), (), s32[]{:S(2)}) async-start(), calls=%async_computation.2 | async-start | bytes 9175040 | tf_op jit(solution)/shard_map/all_gather | solution.py:54
  371.8 230.4 %reduce-scatter.2.cloned.1.call-start = ((), (), s32[]{:S(2)}) async-start(), calls=%async_computation.1 | async-start | bytes 16515072 | tf_op jit(solution)/shard_map/reduce_scatter | solution.py:44
  431.2 0.7 copy-start.9
  431.2 344.9 %all-reduce.9.cloned.1.call-start = ((), (), s32[]{:S(2)}) async-start(), calls=%async_computation.3 | async-start | bytes 14680064 | tf_op jit(solution)/shard_map/psum | solution.py:61
  621.7 1194.3 %all-gather.5.cloned.1.call-start = ((), (), s32[]{:S(2)}) async-start(), calls=%async_computation.4 | async-start | bytes 8257536 | tf_op jit(solution)/shard_map/all_gather | solution.py:63
  791.6 2.9 copy-start.3
  888.4 4.0 copy-start.5
  978.2 1.1 copy-start.4
  1073.5 80.2 %copy-start.7 = (f32[8,128,128]{2,1,0:T(8,128)}, f32[8,128,128]{2,1,0:T(8,128)S(1)}, u32[]{:S(2)}) copy-start(f32[8,128,128]{2,1,0:T(8,128)S(1)} %custom-call.36) | copy-start | bytes 1572868
  1153.8 102.9 %copy-start.6 = (f32[8,128,128]{2,1,0:T(8,128)S(1)}, f32[8,128,128]{2,1,0:T(8,128)}, u32[]{:S(2)}) copy-start(f32[8,128,128]{2,1,0:T(8,128)} %copy-done.5) | copy-start | bytes 1572868
  1394.7 2.9 copy-start.2
  1729.5 4.1 copy-start.8
  1742.4 231.1 %all-reduce.13.cloned.1.call-start = ((), (), s32[]{:S(2)}) async-start(), calls=%async_computation.6 | async-start | bytes 12845056 | tf_op jit(solution)/shard_map/psum | solution.py:14
  1973.5 7.4 copy-start.1
Sparse Core Ops, SparseCore 0:
  70.5 296.7 all-reduce.10
  371.9 78.9 all-gather.2
  453.2 148.9 reduce-scatter.1
  621.9 154.2 all-reduce.8
  1742.5 73.4 all-gather.4
  1836.3 137.0 all-reduce.12
where the time goes:
time: 2000 us; the launch traced here: 1990 us
  other arithmetic  919 us (46%)
  waiting for transfers between devices  829 us (41%)
  matrix products  118 us (6%)
  local copies, waits for them, and re-layouts  102 us (5%)
    another operation x18, other arithmetic, finish(): factor = jnp.linalg.cholesky(gram_matrix)  573 us
    another operation x8, other arithmetic, finish(): lax.linalg.triangular_solve(factor, leaves, left_side=False, lower=True,...  324 us
    unnamed x7, waiting for transfers between devices  295 us
    psum x1, waiting for transfers between devices, local(): gram_matrix = lax.psum(partial_gram, 'col')  153 us
    reduce_scatter x1, waiting for transfers between devices, local(): lax.psum_scatter(own_probe, 'col', scatter_dimension=1, tiled=True)  151 us
    psum x1, waiting for transfers between devices, spread(): return lax.psum(block, axis)  137 us
    all_gather x1, waiting for transfers between devices, local(): whole_basis = lax.all_gather(leaf_basis, 'col', axis=1, tiled=True)  73.5 us
  transfers between devices with their start and end apart: 6, of which 6 were waited for; matrix products, arithmetic and copies ran while one was open for 3% of the time, Pallas kernels for 0%

commit v1 on v0

--- a/solution.py
+++ b/solution.py
@@ -58,7 +58,13 @@
     leaf_count = own_blocks // per_leaf
     leaves = sample.reshape(leaf_count, per_leaf * slab_rows, probes)
     partial_gram = jnp.einsum("lkr,lks->lrs", leaves, leaves, precision=HIGH)
-    gram_matrix = lax.psum(partial_gram, "col")
+    peers = lax.axis_size("col")
+    gram_matrix, far = (partial_gram, 1)
+    while far < peers:
+        gram_matrix = gram_matrix + lax.ppermute(
+            gram_matrix, "col", [(i, i ^ far) for i in range(peers)]
+        )
+        far = 2 * far
     leaf_basis = finish(leaves, gram_matrix).reshape(own_blocks, slab_rows, probes)
     whole_basis = lax.all_gather(leaf_basis, "col", axis=1, tiled=True)
     bases = whole_basis.reshape(leaf_count, LEAF, probes)

time: 2000 us -> 2350 us (1.18)
  waiting for transfers between devices: 829 us -> 1160 us
  other arithmetic: 919 us -> 945 us
    ppermute x0 -> x3, waiting for transfers between devices: none -> 488 us  [local(): lax.ppermute(gram_matrix, 'col', [(i, i ^ far) for i in range(peers)])]
    psum x1 -> x0, waiting for transfers between devices: 153 us -> none  [local(): gram_matrix = lax.psum(partial_gram, 'col')]
    add x0 -> x3, other arithmetic: none -> 25.8 us  [local(): gram_matrix + lax.ppermute(gram_matrix, 'col', [(i, i ^ far) for i in ran...]
    unnamed x7 -> x6, waiting for transfers between devices: 295 us -> 295 us
  transfers between devices with their start and end apart: 6 -> 8, of which waited for: 6 -> 8; matrix products, arithmetic and copies ran while one was open for 3% -> 3% of each run, Pallas kernels for 0% -> 0%
where the time goes in v1:
time: 2350 us
  waiting for transfers between devices  1160 us (49%)
  other arithmetic  945 us (40%)
  matrix products  116 us (5%)
  local copies, waits for them, and re-layouts  103 us (4%)
    another operation x18, other arithmetic, finish(): factor = jnp.linalg.cholesky(gram_matrix)  572 us
    ppermute x3, waiting for transfers between devices, local(): lax.ppermute(gram_matrix, 'col', [(i, i ^ far) for i in range(peers)])  488 us
    another operation x8, other arithmetic, finish(): lax.linalg.triangular_solve(factor, leaves, left_side=False, lower=True,...  324 us
    unnamed x6, waiting for transfers between devices  295 us
    reduce_scatter x1, waiting for transfers between devices, local(): lax.psum_scatter(own_probe, 'col', scatter_dimension=1, tiled=True)  151 us
    psum x1, waiting for transfers between devices, spread(): return lax.psum(block, axis)  137 us
    all_gather x1, waiting for transfers between devices, local(): whole_basis = lax.all_gather(leaf_basis, 'col', axis=1, tiled=True)  71.9 us
  transfers between devices with their start and end apart: 8, of which 8 were waited for; matrix products, arithmetic and copies ran while one was open for 3% of the time, Pallas kernels for 0%

profile of v1, /device:TPU:0, one launch (start us, length us, event | category | flops | bytes accessed | tf_op | source)
XLA Modules:
  0.0 2346.2 jit_solution(4448638083707613202)
XLA Ops:
  16.7 10.6 convolution_bitcast_fusion.1
  37.9 10.9 pad_maximum_fusion
  48.7 21.7 copy.95
  72.3 295.1 %all-reduce.8.cloned.1.call-done = f32[2,28,128,448]{3,0,1,2:T(2,128)} async-done(((f32[2,28,128,448]{3,0,1,2:T(2,128)}), f32[2,28,128,448]{3,0,1,2:T(2,128)}) %all-reduce.8.cloned.1.call-update) | async-done | bytes 12845072
  372.4 30.3 %convolution_bitcast_fusion = f32[56,8,56,128]{3,1,2,0:T(8,128)} fusion(bf16[7168,3584]{1,0:T(8,128)(2,1)} %param.7, bf16[3584,448]{0,1:T(8,128)(2,1)S(1)} %copy-done), kind=kOutput, calls=%fused_computation.11 | convolution fusion | flops 23018340352 | bytes 67436544 | tf_op jit(solution)/shard_map/dot_general | solution.py:34
  402.7 12.1 copy.141
  414.8 16.4 copy.94
  431.9 19.0 all-gather.3.cloned.1.call-done
  450.9 151.3 %reduce-scatter.2.cloned.1.call-done = f32[56,16,448]{2,0,1:T(8,128)} async-done(((f32[56,128,448]{2,0,1:T(8,128)}), f32[56,16,448]{2,0,1:T(8,128)}) %reduce-scatter.2.cloned.1.call-update) | async-done | bytes 1605648 | tf_op jit(solution)/shard_map/reduce_scatter | solution.py:44
  619.9 11.8 collective-permute-done
  639.6 160.2 %collective-permute-done.1 = f32[8,448,448]{1,2,0:T(8,128)S(1)} collective-permute-done((f32[8,448,448]{1,2,0:T(8,128)}, f32[8,448,448]{1,2,0:T(8,128)S(1)}, u32[]{:S(2)}, u32[]{:S(2)}) %collective-permute-start.1) | collective-permute-done | bytes 6422560 | tf_op jit(solution)/shard_map/ppermute | solution.py:64
  809.4 316.0 %collective-permute-done.2 = f32[8,448,448]{1,2,0:T(8,128)} collective-permute-done((f32[8,448,448]{1,2,0:T(8,128)}, f32[8,448,448]{1,2,0:T(8,128)}, u32[]{:S(2)}, u32[]{:S(2)}) %collective-permute-start.2) | collective-permute-done | bytes 6422560 | tf_op jit(solution)/shard_map/ppermute | solution.py:64
  1154.4 93.8 %custom-call.34 = f32[8,128,128]{2,1,0:T(8,128)S(1)} custom-call(f32[8,128,128]{2,1,0:T(8,128)S(1)} %cholesky.281), custom_call_target="Cholesky" | custom-call | tf_op jit(solution)/shard_map/jit(cholesky)/cholesky | solution.py:18
  1252.2 79.2 %custom-call.35 = f32[8,1,128,128]{2,3,1,0:T(8,128)} custom-call(f32[8,1,128,128]{3,2,1,0:T(8,128)S(1)} %select_bitcast_fusion.2), custom_call_target="InvertDiagBlocksLowerTriangular" | custom-call | tf_op jit(solution)/shard_map/jit(cholesky)/cholesky | solution.py:18
  1339.1 94.0 %custom-call.36 = f32[8,128,128]{2,1,0:T(8,128)S(1)} custom-call(f32[8,128,128]{2,1,0:T(8,128)S(1)} %cholesky.285), custom_call_target="Cholesky" | custom-call | tf_op jit(solution)/shard_map/jit(cholesky)/cholesky | solution.py:18
  1434.0 79.2 %custom-call.37 = f32[8,1,128,128]{2,3,1,0:T(8,128)} custom-call(f32[8,1,128,128]{3,2,1,0:T(8,128)S(1)} %get-tuple-element.154), custom_call_target="InvertDiagBlocksLowerTriangular" | custom-call | tf_op jit(solution)/shard_map/jit(cholesky)/cholesky | solution.py:18
  1520.9 95.4 %custom-call.38 = f32[8,128,128]{2,1,0:T(8,128)} custom-call(f32[8,128,128]{2,1,0:T(8,128)} %cholesky.290), custom_call_target="Cholesky" | custom-call | tf_op jit(solution)/shard_map/jit(cholesky)/cholesky | solution.py:18
  1618.6 79.4 %custom-call.39 = f32[8,1,128,128]{2,3,1,0:T(8,128)S(1)} custom-call(f32[8,1,128,128]{3,2,1,0:T(8,128)} %get-tuple-element.152), custom_call_target="InvertDiagBlocksLowerTriangular" | custom-call | tf_op jit(solution)/shard_map/jit(cholesky)/cholesky | solution.py:18
  1701.9 46.9 %custom-call.40 = f32[8,64,64]{2,1,0:T(8,128)S(1)} custom-call(f32[8,64,64]{2,1,0:T(8,128)S(1)} %slice_subtract_fusion.2), custom_call_target="Cholesky" | custom-call | tf_op jit(solution)/shard_map/jit(cholesky)/cholesky | solution.py:18
  1757.2 12.6 while.16
  1773.1 316.1 %custom-call.41 = f32[8,4,128,128]{2,3,1,0:T(8,128)} custom-call(f32[8,4,128,128]{3,2,1,0:T(8,128)} %pad_maximum_fusion.1), custom_call_target="InvertDiagBlocksLowerTriangular" | custom-call | tf_op jit(solution)/shard_map/triangular_solve | solution.py:19
  2102.1 71.9 %all-gather.5.cloned.1.call-done = bf16[56,128,448]{2,1,0:T(8,128)(2,1)} async-done(((bf16[56,16,448]{2,1,0:T(8,128)(2,1)}), bf16[56,128,448]{2,1,0:T(8,128)(2,1)}) %all-gather.5.cloned.1.call-update) | async-done | bytes 6422544 | tf_op jit(solution)/shard_map/all_gather | solution.py:69
  2174.0 17.3 while.15
  2194.5 137.2 %all-reduce.10.cloned.1.call-done = (bf16[4,896,448]{1,2,0:T(8,128)(2,1)}, bf16[4,896,448]{1,2,0:T(8,128)(2,1)}) async-done(((bf16[4,896,448]{1,2,0:T(8,128)(2,1)}, bf16[4,896,448]{1,2,0:T(8,128)(2,1)}), (bf16[4,896,448]{1,2,0:T(8,128)(2,1)}, bf16[4,896,448]{1,2,0:T(8,128)(2,1)})) %all-reduce.10.cloned.1.call-update) | async-done | bytes 6422544 | tf_op jit(solution)/shard_map/psum | solution.py:14
  (112 shorter events, 179.1 us)
Async XLA Ops:
  7.2 365.2 %copy-start = (bf16[3584,448]{0,1:T(8,128)(2,1)S(1)}, bf16[3584,448]{0,1:T(8,128)(2,1)}, u32[]{:S(2)}) copy-start(bf16[3584,448]{0,1:T(8,128)(2,1)} %param.9) | copy-start | bytes 9633796
  7.2 360.2 %all-reduce.8.cloned.1.call-start = ((), (), s32[]{:S(2)}) async-start(), calls=%async_computation.4 | async-start | bytes 29360128
  70.4 0.7 copy-start.10
  70.4 380.5 %all-gather.3.cloned.1.call-start = ((), (), s32[]{:S(2)}) async-start(), calls=%async_computation.2 | async-start | bytes 9175040 | tf_op jit(solution)/shard_map/all_gather | solution.py:54
  371.8 230.4 %reduce-scatter.2.cloned.1.call-start = ((), (), s32[]{:S(2)}) async-start(), calls=%async_computation.1 | async-start | bytes 16515072 | tf_op jit(solution)/shard_map/reduce_scatter | solution.py:44
  431.2 0.7 copy-start.9
  431.2 1742.8 %all-gather.5.cloned.1.call-start = ((), (), s32[]{:S(2)}) async-start(), calls=%async_computation.3 | async-start | bytes 8257536 | tf_op jit(solution)/shard_map/all_gather | solution.py:69
  619.9 11.9 collective-permute-start
  639.6 160.2 %collective-permute-start.1 = (f32[8,448,448]{1,2,0:T(8,128)}, f32[8,448,448]{1,2,0:T(8,128)S(1)}, u32[]{:S(2)}, u32[]{:S(2)}) collective-permute-start(f32[8,448,448]{1,2,0:T(8,128)} %add.112), channel_id=1, source_target_pairs={{0,2},{1,3},{2,0},{3,1},{4,6},{5,7},{6,4},{7,5},{8,10},{9,11},{10,... | collective-permute-start | bytes 19267592 | tf_op jit(solution)/shard_map/ppermute | solution.py:64
  807.8 317.7 %collective-permute-start.2 = (f32[8,448,448]{1,2,0:T(8,128)}, f32[8,448,448]{1,2,0:T(8,128)}, u32[]{:S(2)}, u32[]{:S(2)}) collective-permute-start(f32[8,448,448]{1,2,0:T(8,128)} %add.113), channel_id=1, source_target_pairs={{0,4},{1,5},{2,6},{3,7},{4,0},{5,1},{6,2},{7,3},{8,12},{9,13},{10,... | collective-permute-start | bytes 19267592 | tf_op jit(solution)/shard_map/ppermute | solution.py:64
  1151.4 2.9 copy-start.3
  1248.2 4.0 copy-start.5
  1337.9 1.1 copy-start.4
  1433.0 80.2 %copy-start.7 = (f32[8,128,128]{2,1,0:T(8,128)}, f32[8,128,128]{2,1,0:T(8,128)S(1)}, u32[]{:S(2)}) copy-start(f32[8,128,128]{2,1,0:T(8,128)S(1)} %custom-call.36) | copy-start | bytes 1572868
  1513.2 103.1 %copy-start.6 = (f32[8,128,128]{2,1,0:T(8,128)S(1)}, f32[8,128,128]{2,1,0:T(8,128)}, u32[]{:S(2)}) copy-start(f32[8,128,128]{2,1,0:T(8,128)} %copy-done.5) | copy-start | bytes 1572868
  1754.2 2.9 copy-start.2
  2089.1 4.1 copy-start.8
  2102.1 229.7 %all-reduce.10.cloned.1.call-start = ((), (), s32[]{:S(2)}) async-start(), calls=%async_computation.5 | async-start | bytes 12845056 | tf_op jit(solution)/shard_map/psum | solution.py:14
  2331.8 7.4 copy-start.1
Sparse Core Ops, SparseCore 0:
  70.6 296.7 all-reduce.7
  371.9 78.9 all-gather.2
  453.2 148.9 reduce-scatter.1
  2102.2 71.7 all-gather.4
  2194.6 137.0 all-reduce.9
